TPU v7x, 256 devices: a whole 4x4x8 slice. The times are simulated.
256 devices in a mesh: lx: 8 (over z), ly: 8 (over x, y_lo), blk: 4 (over y_hi, core).
Axes of the slice: x: 4, y: 4 (y_hi: 2, y_lo: 2; y = y_hi * 2 + y_lo), z: 8, core: 2. Of those that a mesh axis runs over, the one named last changes fastest.
Arguments:
- block_vectors: float32 [32, 1024, 2048], P('blk', 'lx', 'ly'), may hold values from -6 to 6
- search_vectors: float32 [256, 1024, 2048], P('blk', 'lx', 'ly'), may hold values from -6 to 6
- onsite_energy: float32 [1024, 2048], P('lx', 'ly'), may hold values from -1 to 1
- site_mask: int32 [1024, 2048], P('lx', 'ly'), may hold values 0 or 1
- filter_coefs: float32 [5], replicated, may hold values from -1 to 1
Outputs:
- projected: float32 [2, 32, 256], P(None, None, 'blk')
Inputs may be any that keep to these rules, and one draw needn't show every extreme that they name: `site_mask`: 1 marks a present site, 0 a vacancy.
All inputs are finite; a program needn't handle non-finite values. No bound on the sum of `site_mask` on one device may be relied on, other than what follows from the above.
Results may differ from a plain program's by a relative error of at most 0.00016.
Values sent between devices are 32-bit elements; how exact they have to be, the bound alone decides.
No kernel may reach another device: no remote copies, remote signals or barrier semaphores. Data moves between devices by JAX's collectives and lax.ppermute only.
A program may use at most 64 MiB of HBM per device.

v0:
```python
import math
import jax
import jax.numpy as jnp
from jax import lax
from jax.sharding import PartitionSpec as P


def extended(block, sides, width):
    for axis, dim in sides:
        count = lax.axis_size(axis)
        forward = [(i, i + 1) for i in range(count - 1)]
        backward = [(target, source) for source, target in forward]
        low = lax.ppermute(
            lax.slice_in_dim(block, block.shape[dim] - width, None, axis=dim), axis, forward
        )
        high = lax.ppermute(lax.slice_in_dim(block, 0, width, axis=dim), axis, backward)
        block = jnp.concatenate([low, block, high], axis=dim)
    return block


def scaled_step(padded, onsite, present):
    nrows, ncols = onsite.shape
    row_index = lax.broadcasted_iota(jnp.int32, (nrows, ncols), 0)
    col_index = lax.broadcasted_iota(jnp.int32, (nrows, ncols), 1)
    even_sites = (row_index + col_index) % 2 == 0
    centre = padded[..., 1:-1, 1:-1]
    left_side = padded[..., 1:-1, :-2]
    right_side = padded[..., 1:-1, 2:]
    upper_side = padded[..., :-2, 1:-1]
    lower_side = padded[..., 2:, 1:-1]
    vertical = jnp.where(even_sites, lower_side, upper_side)
    return present * (onsite * centre - (left_side + right_side + vertical)) * 0.25


def gram_rows(stacked, search_vectors):
    stacks, members, nrows, ncols = stacked.shape
    flat = stacked.reshape(stacks * members, nrows * ncols)
    search_flat = search_vectors.reshape(search_vectors.shape[0], nrows * ncols)
    result = lax.dot_general(
        flat,
        search_flat,
        (((1,), (1,)), ((), ())),
        precision=lax.Precision.HIGHEST,
        preferred_element_type=jnp.float32,
    )
    return result.reshape(stacks, members, search_vectors.shape[0])


def shards(block_vectors, search_vectors, onsite_energy, site_mask, filter_coefs):
    present = site_mask.astype(jnp.float32)
    current = block_vectors * present
    filtered = filter_coefs[0] * current
    degree = filter_coefs.shape[0] - 1
    before = current
    for order in range(1, degree + 1):
        padded_field = extended(current, (("lx", 1), ("ly", 2)), 1)
        image = scaled_step(padded_field, onsite_energy, present)
        following = image if order == 1 else 2.0 * image - before
        before, current = (current, following)
        filtered = filtered + filter_coefs[order] * current
    nrows, ncols = onsite_energy.shape
    scale_factor = 1.0 / math.sqrt(nrows * ncols * lax.axis_size("lx") * lax.axis_size("ly"))
    padded_field = extended(filtered, (("lx", 1), ("ly", 2)), 1)
    image = scaled_step(padded_field, onsite_energy, present)
    paired = jnp.stack([filtered, image])
    partial_gram = gram_rows(lax.all_gather(paired, "blk", axis=1, tiled=True), search_vectors)
    total = lax.psum(partial_gram, ("lx", "ly"))
    return total * scale_factor


def solution(mesh):
    placed = (P("blk", "lx", "ly"), P("blk", "lx", "ly"), P("lx", "ly"), P("lx", "ly"), P())
    return jax.shard_map(
        shards, mesh=mesh, in_specs=placed, out_specs=P(None, None, "blk"), check_vma=False
    )
```

profile of v0, /device:TPU:16, one launch (start us, length us, event | category | flops | bytes accessed | tf_op | source)
XLA Modules:
  0.0 537.4 jit_solution(5126460402475514423)
XLA Ops:
  6.5 0.9 convert_element_type.3
  7.5 1.8 copy_multiply_fusion
  9.3 1.3 collective-permute-start.1
  10.6 4.5 collective-permute-start
  15.2 1.3 collective-permute-done
  17.1 0.4 copy.11
  17.5 1.3 collective-permute-start.3
  18.8 4.5 collective-permute-start.2
  23.4 1.3 collective-permute-done.2
  24.7 1.2 copy.10
  25.9 1.2 copy.12
  27.1 1.9 broadcast_multiply_fusion
  29.0 1.3 collective-permute-start.5
  30.3 4.8 collective-permute-start.4
  35.2 1.3 collective-permute-done.4
  36.6 1.0 fusion.50
  37.6 1.4 copy.13
  39.0 0.4 copy.15
  39.3 1.3 collective-permute-start.7
  40.6 4.8 collective-permute-start.6
  45.5 0.7 broadcast_multiply_fusion.1
  46.1 0.7 collective-permute-done.6
  46.8 1.2 copy.14
  48.0 1.2 copy.16
  49.2 2.6 fusion.34
  51.8 1.3 collective-permute-start.9
  53.1 4.8 collective-permute-start.8
  58.0 1.3 collective-permute-done.8
  59.4 1.0 fusion.49
  60.4 1.4 copy.17
  61.8 5.0 collective-permute-start.10
  67.1 1.3 collective-permute-start.11
  68.4 0.4 copy.18
  68.8 5.0 collective-permute-done.11
  73.8 1.2 copy.20
  75.0 1.8 fusion.27
  76.8 1.3 collective-permute-start.13
  78.1 4.9 collective-permute-start.12
  83.1 1.3 collective-permute-done.12
  84.5 1.0 fusion.48
  85.5 1.4 copy.21
  86.9 0.4 copy.23
  87.2 1.3 collective-permute-start.15
  88.5 5.4 %collective-permute-start.14 = (f32[8,130,1]{1,0,2:T(8,128)S(1)}, f32[8,130,1]{1,0,2:T(8,128)S(1)}, u32[]{:S(2)}, u32[]{:S(2)}) collective-permute-start(f32[8,130,1]{1,0,2:T(8,128)S(1)} %copy.21), channel_id=1, source_target_pairs={{0,4},{4,8},{8,12},{12,16},{16,20},{20,24},{24,28},{1,5},{5,9},{9,... | collective-permute-start | bytes 12488 | tf_op jit(solution)/shard_map/ppermute | solution.py:13
  94.0 0.7 fusion.57
  95.3 1.2 copy.22
  96.5 1.2 copy.24
  97.7 8.3 %fusion.20 = f32[8,128,256]{2,0,1:T(8,128)S(1)} fusion(f32[8,128,256]{2,0,1:T(8,128)S(1)} %fusion.34, f32[8,128,256]{2,0,1:T(8,128)} %copy-done, f32[8,1,256]{2,0,1:T(8,128)S(1)} %collective-permute-done.12, f32[8,1,256]{2,0,1:T(8,128)S(1)} %collective-permute-done.13, f32[8,130,1]{2,0,1:T(8,128)} %copy.24, f32[8,130,1]{2,0,1:T(8,128)} %copy.22, ...), kind=kLoop, calls=%fused_computation.33 | loop fusion | flops 6815744 | bytes 5562516 | tf_op jit(solution)/shard_map/add | solution.py:60
  106.0 1.3 collective-permute-start.17
  107.3 6.0 %collective-permute-start.16 = (f32[8,1,256]{2,0,1:T(8,128)S(1)}, f32[8,1,256]{2,0,1:T(8,128)S(1)}, u32[]{:S(2)}, u32[]{:S(2)}) collective-permute-start(f32[8,1,256]{2,0,1:T(8,128)S(1)} %get-tuple-element.18), channel_id=1, source_target_pairs={{0,32},{32,64},{64,96},{96,128},{128,160},{160,192},{192,224},{1,3... | collective-permute-start | bytes 24584 | tf_op jit(solution)/shard_map/ppermute | solution.py:13
  113.3 1.3 collective-permute-done.16
  115.0 0.4 copy.25
  115.3 4.8 collective-permute-start.18
  120.1 0.3 copy.27
  120.5 1.5 collective-permute-start.19
  122.0 0.4 copy.26
  122.4 4.8 collective-permute-done.19
  127.2 1.2 copy.28
  128.4 1.8 fusion.11
  130.2 1.5 pad_maximum_fusion
  131.7 71.7 %all-gather.2.cloned.1.call-done = f32[2,32,128,256]{3,1,2,0:T(8,128)} async-done(((f32[2,8,128,256]{3,1,2,0:T(8,128)}), f32[2,32,128,256]{3,1,2,0:T(8,128)}) %all-gather.2.cloned.1.call-update) | async-done | bytes 8388624 | tf_op jit(solution)/shard_map/all_gather | solution.py:66
  203.4 16.7 %fusion.3 = f32[2,32,64]{2,1,0:T(8,128)S(1)} fusion(f32[2,32,128,256]{3,1,2,0:T(8,128)} %all-gather.2.cloned.1.call-done, f32[64,128,256]{2,1,0:T(8,128)} %param.6), kind=kOutput, calls=%fused_computation.4 | convolution fusion | flops 1610612736 | bytes 16793600 | tf_op jit(solution)/shard_map/dot_general | solution.py:39
  220.0 309.9 %psum.7 = f32[2,32,64]{2,1,0:T(8,128)S(1)} all-reduce(f32[2,32,64]{2,1,0:T(8,128)S(1)} %fusion.3), channel_id=1, replica_groups=mesh['lx'=8,'ly'=8,'blk'=4] {'lx','ly'}, use_global_device_ids=true, to_apply=%region_0.1 | all-reduce | flops 4096 | bytes 32768 | tf_op jit(solution)/shard_map/psum | solution.py:67
  529.9 0.6 broadcast_multiply_fusion.2
  (34 shorter events, 1.7 us)
Async XLA Ops:
  6.5 196.8 %all-gather.2.cloned.1.call-start = ((), (), s32[]{:S(2)}) async-start(), calls=%async_computation | async-start | bytes 10485760 | tf_op jit(solution)/shard_map/all_gather | solution.py:66
  9.3 5.9 %collective-permute-start.1 = (f32[8,1,256]{2,0,1:T(8,128)S(1)}, f32[8,1,256]{2,0,1:T(8,128)S(1)}, u32[]{:S(2)}, u32[]{:S(2)}) collective-permute-start(f32[8,1,256]{2,0,1:T(8,128)S(1)} %get-tuple-element.25), channel_id=1, source_target_pairs={{32,0},{64,32},{96,64},{128,96},{160,128},{192,160},{224,192},{33,... | collective-permute-start | bytes 24584 | tf_op jit(solution)/shard_map/ppermute | solution.py:16
  10.6 5.9 %collective-permute-start = (f32[8,1,256]{2,0,1:T(8,128)S(1)}, f32[8,1,256]{2,0,1:T(8,128)S(1)}, u32[]{:S(2)}, u32[]{:S(2)}) collective-permute-start(f32[8,1,256]{2,0,1:T(8,128)S(1)} %get-tuple-element.26), channel_id=1, source_target_pairs={{0,32},{32,64},{64,96},{96,128},{128,160},{160,192},{192,224},{1,3... | collective-permute-start | bytes 24584 | tf_op jit(solution)/shard_map/ppermute | solution.py:13
  16.8 10.3 %copy-start.1 = (f32[128,256]{1,0:T(8,128)S(1)}, f32[128,256]{1,0:T(8,128)}, u32[]{:S(2)}) copy-start(f32[128,256]{1,0:T(8,128)} %param.7) | copy-start | bytes 393220
  17.5 8.4 %collective-permute-start.3 = (f32[8,130,1]{1,0,2:T(8,128)S(1)}, f32[8,130,1]{1,0,2:T(8,128)S(1)}, u32[]{:S(2)}, u32[]{:S(2)}) collective-permute-start(f32[8,130,1]{1,0,2:T(8,128)S(1)} %copy.11), channel_id=1, source_target_pairs={{4,0},{8,4},{12,8},{16,12},{20,16},{24,20},{28,24},{5,1},{9,5},{13... | collective-permute-start | bytes 12488 | tf_op jit(solution)/shard_map/ppermute | solution.py:16
  18.8 5.9 %collective-permute-start.2 = (f32[8,130,1]{1,0,2:T(8,128)S(1)}, f32[8,130,1]{1,0,2:T(8,128)S(1)}, u32[]{:S(2)}, u32[]{:S(2)}) collective-permute-start(f32[8,130,1]{1,0,2:T(8,128)S(1)} %copy.9), channel_id=1, source_target_pairs={{0,4},{4,8},{8,12},{12,16},{16,20},{20,24},{24,28},{1,5},{5,9},{9,... | collective-permute-start | bytes 12488 | tf_op jit(solution)/shard_map/ppermute | solution.py:13
  29.0 6.1 %collective-permute-start.5 = (f32[8,1,256]{2,0,1:T(8,128)S(1)}, f32[8,1,256]{2,0,1:T(8,128)S(1)}, u32[]{:S(2)}, u32[]{:S(2)}) collective-permute-start(f32[8,1,256]{2,0,1:T(8,128)S(1)} %get-tuple-element.23), channel_id=1, source_target_pairs={{32,0},{64,32},{96,64},{128,96},{160,128},{192,160},{224,192},{33,... | collective-permute-start | bytes 24584 | tf_op jit(solution)/shard_map/ppermute | solution.py:16
  30.3 6.2 %collective-permute-start.4 = (f32[8,1,256]{2,0,1:T(8,128)S(1)}, f32[8,1,256]{2,0,1:T(8,128)S(1)}, u32[]{:S(2)}, u32[]{:S(2)}) collective-permute-start(f32[8,1,256]{2,0,1:T(8,128)S(1)} %get-tuple-element.24), channel_id=1, source_target_pairs={{0,32},{32,64},{64,96},{96,128},{128,160},{160,192},{192,224},{1,3... | collective-permute-start | bytes 24584 | tf_op jit(solution)/shard_map/ppermute | solution.py:13
  39.3 8.7 %collective-permute-start.7 = (f32[8,130,1]{1,0,2:T(8,128)S(1)}, f32[8,130,1]{1,0,2:T(8,128)S(1)}, u32[]{:S(2)}, u32[]{:S(2)}) collective-permute-start(f32[8,130,1]{1,0,2:T(8,128)S(1)} %copy.15), channel_id=1, source_target_pairs={{4,0},{8,4},{12,8},{16,12},{20,16},{24,20},{28,24},{5,1},{9,5},{13... | collective-permute-start | bytes 12488 | tf_op jit(solution)/shard_map/ppermute | solution.py:16
  40.6 6.2 %collective-permute-start.6 = (f32[8,130,1]{1,0,2:T(8,128)S(1)}, f32[8,130,1]{1,0,2:T(8,128)S(1)}, u32[]{:S(2)}, u32[]{:S(2)}) collective-permute-start(f32[8,130,1]{1,0,2:T(8,128)S(1)} %copy.13), channel_id=1, source_target_pairs={{0,4},{4,8},{8,12},{12,16},{16,20},{20,24},{24,28},{1,5},{5,9},{9,... | collective-permute-start | bytes 12488 | tf_op jit(solution)/shard_map/ppermute | solution.py:13
  51.8 6.1 %collective-permute-start.9 = (f32[8,1,256]{2,0,1:T(8,128)S(1)}, f32[8,1,256]{2,0,1:T(8,128)S(1)}, u32[]{:S(2)}, u32[]{:S(2)}) collective-permute-start(f32[8,1,256]{2,0,1:T(8,128)S(1)} %get-tuple-element.21), channel_id=1, source_target_pairs={{32,0},{64,32},{96,64},{128,96},{160,128},{192,160},{224,192},{33,... | collective-permute-start | bytes 24584 | tf_op jit(solution)/shard_map/ppermute | solution.py:16
  53.1 6.2 %collective-permute-start.8 = (f32[8,1,256]{2,0,1:T(8,128)S(1)}, f32[8,1,256]{2,0,1:T(8,128)S(1)}, u32[]{:S(2)}, u32[]{:S(2)}) collective-permute-start(f32[8,1,256]{2,0,1:T(8,128)S(1)} %get-tuple-element.22), channel_id=1, source_target_pairs={{0,32},{32,64},{64,96},{96,128},{128,160},{160,192},{192,224},{1,3... | collective-permute-start | bytes 24584 | tf_op jit(solution)/shard_map/ppermute | solution.py:13
  61.8 6.6 %collective-permute-start.10 = (f32[8,130,1]{1,0,2:T(8,128)S(1)}, f32[8,130,1]{1,0,2:T(8,128)S(1)}, u32[]{:S(2)}, u32[]{:S(2)}) collective-permute-start(f32[8,130,1]{1,0,2:T(8,128)S(1)} %copy.17), channel_id=1, source_target_pairs={{0,4},{4,8},{8,12},{12,16},{16,20},{20,24},{24,28},{1,5},{5,9},{9,... | collective-permute-start | bytes 12488 | tf_op jit(solution)/shard_map/ppermute | solution.py:13
  67.1 6.7 %collective-permute-start.11 = (f32[8,130,1]{1,0,2:T(8,128)S(1)}, f32[8,130,1]{1,0,2:T(8,128)S(1)}, u32[]{:S(2)}, u32[]{:S(2)}) collective-permute-start(f32[8,130,1]{1,0,2:T(8,128)S(1)} %copy.19), channel_id=1, source_target_pairs={{4,0},{8,4},{12,8},{16,12},{20,16},{24,20},{28,24},{5,1},{9,5},{13... | collective-permute-start | bytes 12488 | tf_op jit(solution)/shard_map/ppermute | solution.py:16
  76.8 7.7 %copy-start = (f32[8,128,256]{2,0,1:T(8,128)}, f32[8,128,256]{2,0,1:T(8,128)S(1)}, u32[]{:S(2)}) copy-start(f32[8,128,256]{2,0,1:T(8,128)S(1)} %fusion.27) | copy-start | bytes 3145732
  76.8 6.2 %collective-permute-start.13 = (f32[8,1,256]{2,0,1:T(8,128)S(1)}, f32[8,1,256]{2,0,1:T(8,128)S(1)}, u32[]{:S(2)}, u32[]{:S(2)}) collective-permute-start(f32[8,1,256]{2,0,1:T(8,128)S(1)} %get-tuple-element.19), channel_id=1, source_target_pairs={{32,0},{64,32},{96,64},{128,96},{160,128},{192,160},{224,192},{33,... | collective-permute-start | bytes 24584 | tf_op jit(solution)/shard_map/ppermute | solution.py:16
  78.1 6.3 %collective-permute-start.12 = (f32[8,1,256]{2,0,1:T(8,128)S(1)}, f32[8,1,256]{2,0,1:T(8,128)S(1)}, u32[]{:S(2)}, u32[]{:S(2)}) collective-permute-start(f32[8,1,256]{2,0,1:T(8,128)S(1)} %get-tuple-element.20), channel_id=1, source_target_pairs={{0,32},{32,64},{64,96},{96,128},{128,160},{160,192},{192,224},{1,3... | collective-permute-start | bytes 24584 | tf_op jit(solution)/shard_map/ppermute | solution.py:13
  85.5 8.5 %copy-start.2 = (f32[5]{0:T(128)S(1)}, f32[5]{0:T(128)}, u32[]{:S(2)}) copy-start(f32[5]{0:T(128)} %param.9) | copy-start | bytes 64
  87.2 9.3 %collective-permute-start.15 = (f32[8,130,1]{1,0,2:T(8,128)S(1)}, f32[8,130,1]{1,0,2:T(8,128)S(1)}, u32[]{:S(2)}, u32[]{:S(2)}) collective-permute-start(f32[8,130,1]{1,0,2:T(8,128)S(1)} %copy.23), channel_id=1, source_target_pairs={{4,0},{8,4},{12,8},{16,12},{20,16},{24,20},{28,24},{5,1},{9,5},{13... | collective-permute-start | bytes 12488 | tf_op jit(solution)/shard_map/ppermute | solution.py:16
  88.5 6.8 %collective-permute-start.14 = (f32[8,130,1]{1,0,2:T(8,128)S(1)}, f32[8,130,1]{1,0,2:T(8,128)S(1)}, u32[]{:S(2)}, u32[]{:S(2)}) collective-permute-start(f32[8,130,1]{1,0,2:T(8,128)S(1)} %copy.21), channel_id=1, source_target_pairs={{0,4},{4,8},{8,12},{12,16},{16,20},{20,24},{24,28},{1,5},{5,9},{9,... | collective-permute-start | bytes 12488 | tf_op jit(solution)/shard_map/ppermute | solution.py:13
  106.0 7.3 %collective-permute-start.17 = (f32[8,1,256]{2,0,1:T(8,128)S(1)}, f32[8,1,256]{2,0,1:T(8,128)S(1)}, u32[]{:S(2)}, u32[]{:S(2)}) collective-permute-start(f32[8,1,256]{2,0,1:T(8,128)S(1)} %get-tuple-element.17), channel_id=1, source_target_pairs={{32,0},{64,32},{96,64},{128,96},{160,128},{192,160},{224,192},{33,... | collective-permute-start | bytes 24584 | tf_op jit(solution)/shard_map/ppermute | solution.py:16
  107.3 7.4 %collective-permute-start.16 = (f32[8,1,256]{2,0,1:T(8,128)S(1)}, f32[8,1,256]{2,0,1:T(8,128)S(1)}, u32[]{:S(2)}, u32[]{:S(2)}) collective-permute-start(f32[8,1,256]{2,0,1:T(8,128)S(1)} %get-tuple-element.18), channel_id=1, source_target_pairs={{0,32},{32,64},{64,96},{96,128},{128,160},{160,192},{192,224},{1,3... | collective-permute-start | bytes 24584 | tf_op jit(solution)/shard_map/ppermute | solution.py:13
  115.3 6.7 %collective-permute-start.18 = (f32[8,130,1]{1,0,2:T(8,128)S(1)}, f32[8,130,1]{1,0,2:T(8,128)S(1)}, u32[]{:S(2)}, u32[]{:S(2)}) collective-permute-start(f32[8,130,1]{1,0,2:T(8,128)S(1)} %copy.25), channel_id=1, source_target_pairs={{0,4},{4,8},{8,12},{12,16},{16,20},{20,24},{24,28},{1,5},{5,9},{9,... | collective-permute-start | bytes 12488 | tf_op jit(solution)/shard_map/ppermute | solution.py:13
  120.5 6.7 %collective-permute-start.19 = (f32[8,130,1]{1,0,2:T(8,128)S(1)}, f32[8,130,1]{1,0,2:T(8,128)S(1)}, u32[]{:S(2)}, u32[]{:S(2)}) collective-permute-start(f32[8,130,1]{1,0,2:T(8,128)S(1)} %copy.27), channel_id=1, source_target_pairs={{4,0},{8,4},{12,8},{16,12},{20,16},{24,20},{28,24},{5,1},{9,5},{13... | collective-permute-start | bytes 12488 | tf_op jit(solution)/shard_map/ppermute | solution.py:16
Sparse Core Ops, SparseCore 0:
  131.8 71.4 all-gather.1
where the time goes:
time: 538 us; the launch traced here: 537 us
  blocking collectives  310 us (58%)
  waiting for transfers between devices  90.3 us (17%)
  starting transfers between devices  62.9 us (12%)
  other arithmetic  22.4 us (4%)
  local copies, waits for them, and re-layouts  20.9 us (4%)
  matrix products  16.7 us (3%)
  between operations  14.3 us (3%)
    psum x1, blocking collectives, shards(): total = lax.psum(partial_gram, ('lx', 'ly'))  310 us
    all_gather x1, waiting for transfers between devices, shards(): lax.all_gather(paired, 'blk', axis=1, tiled=True)  71.7 us
    ppermute x10, starting transfers between devices, extended(): lax.ppermute(lax.slice_in_dim(block, block.shape[dim] - width, None, axis...  49.7 us
    dot_general x1, matrix products, gram_rows(): lax.dot_general(flat, search_flat, (((1,), (1,)), ((), ())), precision=la...  16.7 us
    ppermute x10, starting transfers between devices, extended(): lax.ppermute(lax.slice_in_dim(block, 0, width, axis=dim), axis, backward)  13.1 us
  transfers between devices with their start and end apart: 21, of which 11 were waited for; matrix products, arithmetic and copies ran while one was open for 1% of the time, Pallas kernels for 0%

commit v1 on v0

--- a/solution.py
+++ b/solution.py
@@ -64,7 +64,7 @@
     image = scaled_step(padded_field, onsite_energy, present)
     paired = jnp.stack([filtered, image])
     partial_gram = gram_rows(lax.all_gather(paired, "blk", axis=1, tiled=True), search_vectors)
-    total = lax.psum(partial_gram, ("lx", "ly"))
+    total = lax.psum(lax.psum(partial_gram, "ly"), "lx")
     return total * scale_factor
 
 

time: 538 us -> 294 us (0.55)
  blocking collectives: 310 us -> 65.1 us
    psum x1 -> x2, blocking collectives: 310 us -> 65.1 us  [shards(): total = lax.psum(lax.psum(partial_gram, 'ly'), 'lx')]
  transfers between devices with their start and end apart: 21 -> 21, of which waited for: 11 -> 10; matrix products, arithmetic and copies ran while one was open for 1% -> 2% of each run, Pallas kernels for 0% -> 0%
where the time goes in v1:
time: 294 us; the launch traced here: 293 us
  waiting for transfers between devices  90.2 us (31%)
  blocking collectives  65.1 us (22%)
  starting transfers between devices  62.9 us (21%)
  other arithmetic  22.4 us (8%)
  local copies, waits for them, and re-layouts  21 us (7%)
  matrix products  16.7 us (6%)
  between operations  14.4 us (5%)
    all_gather x1, waiting for transfers between devices, shards(): lax.all_gather(paired, 'blk', axis=1, tiled=True)  71.7 us
    psum x2, blocking collectives, shards(): total = lax.psum(lax.psum(partial_gram, 'ly'), 'lx')  65.1 us
    ppermute x10, starting transfers between devices, extended(): lax.ppermute(lax.slice_in_dim(block, block.shape[dim] - width, None, axis...  49.7 us
    dot_general x1, matrix products, gram_rows(): lax.dot_general(flat, search_flat, (((1,), (1,)), ((), ())), precision=la...  16.7 us
    ppermute x10, starting transfers between devices, extended(): lax.ppermute(lax.slice_in_dim(block, 0, width, axis=dim), axis, backward)  13.1 us
    ppermute x10, waiting for transfers between devices, extended(): lax.ppermute(lax.slice_in_dim(block, 0, width, axis=dim), axis, backward)  9.85 us
    ppermute x10, waiting for transfers between devices, extended(): lax.ppermute(lax.slice_in_dim(block, block.shape[dim] - width, None, axis...  8.71 us
    add x1, other arithmetic, shards(): filtered = filtered + filter_coefs[order] * current  8.34 us
  transfers between devices with their start and end apart: 21, of which 10 were waited for; matrix products, arithmetic and copies ran while one was open for 2% of the time, Pallas kernels for 0%

profile of v1, /device:TPU:16, one launch (start us, length us, event | category | flops | bytes accessed | tf_op | source)
XLA Modules:
  0.0 292.8 jit_solution(8926001301729085874)
XLA Ops:
  6.5 0.9 convert_element_type.3
  7.5 1.8 copy_multiply_fusion
  9.3 1.3 collective-permute-start.1
  10.6 4.5 %collective-permute-start = (f32[8,1,256]{2,0,1:T(8,128)S(1)}, f32[8,1,256]{2,0,1:T(8,128)S(1)}, u32[]{:S(2)}, u32[]{:S(2)}) collective-permute-start(f32[8,1,256]{2,0,1:T(8,128)S(1)} %get-tuple-element.26), channel_id=1, source_target_pairs={{0,32},{32,64},{64,96},{96,128},{128,160},{160,192},{192,224},{1,3... | collective-permute-start | bytes 24584 | tf_op jit(solution)/shard_map/ppermute | solution.py:13
  15.2 1.3 collective-permute-done
  17.1 0.4 copy.11
  17.5 1.3 collective-permute-start.3
  18.8 4.5 %collective-permute-start.2 = (f32[8,130,1]{1,0,2:T(8,128)S(1)}, f32[8,130,1]{1,0,2:T(8,128)S(1)}, u32[]{:S(2)}, u32[]{:S(2)}) collective-permute-start(f32[8,130,1]{1,0,2:T(8,128)S(1)} %copy.9), channel_id=1, source_target_pairs={{0,4},{4,8},{8,12},{12,16},{16,20},{20,24},{24,28},{1,5},{5,9},{9,... | collective-permute-start | bytes 12488 | tf_op jit(solution)/shard_map/ppermute | solution.py:13
  23.4 1.3 collective-permute-done.2
  24.7 1.2 copy.10
  25.9 1.2 copy.12
  27.1 1.9 broadcast_multiply_fusion
  29.1 1.3 collective-permute-start.5
  30.4 4.8 %collective-permute-start.4 = (f32[8,1,256]{2,0,1:T(8,128)S(1)}, f32[8,1,256]{2,0,1:T(8,128)S(1)}, u32[]{:S(2)}, u32[]{:S(2)}) collective-permute-start(f32[8,1,256]{2,0,1:T(8,128)S(1)} %get-tuple-element.24), channel_id=1, source_target_pairs={{0,32},{32,64},{64,96},{96,128},{128,160},{160,192},{192,224},{1,3... | collective-permute-start | bytes 24584 | tf_op jit(solution)/shard_map/ppermute | solution.py:13
  35.2 1.3 collective-permute-done.4
  36.6 1.0 fusion.50
  37.6 1.4 copy.13
  39.0 0.4 copy.15
  39.4 1.3 collective-permute-start.7
  40.7 4.8 %collective-permute-start.6 = (f32[8,130,1]{1,0,2:T(8,128)S(1)}, f32[8,130,1]{1,0,2:T(8,128)S(1)}, u32[]{:S(2)}, u32[]{:S(2)}) collective-permute-start(f32[8,130,1]{1,0,2:T(8,128)S(1)} %copy.13), channel_id=1, source_target_pairs={{0,4},{4,8},{8,12},{12,16},{16,20},{20,24},{24,28},{1,5},{5,9},{9,... | collective-permute-start | bytes 12488 | tf_op jit(solution)/shard_map/ppermute | solution.py:13
  45.5 0.7 broadcast_multiply_fusion.1
  46.1 0.7 collective-permute-done.6
  46.8 1.2 copy.14
  48.0 1.2 copy.16
  49.2 2.6 fusion.34
  51.8 1.3 collective-permute-start.9
  53.1 4.8 %collective-permute-start.8 = (f32[8,1,256]{2,0,1:T(8,128)S(1)}, f32[8,1,256]{2,0,1:T(8,128)S(1)}, u32[]{:S(2)}, u32[]{:S(2)}) collective-permute-start(f32[8,1,256]{2,0,1:T(8,128)S(1)} %get-tuple-element.22), channel_id=1, source_target_pairs={{0,32},{32,64},{64,96},{96,128},{128,160},{160,192},{192,224},{1,3... | collective-permute-start | bytes 24584 | tf_op jit(solution)/shard_map/ppermute | solution.py:13
  58.0 1.3 collective-permute-done.8
  59.4 1.0 fusion.49
  60.4 1.4 copy.17
  61.8 5.0 %collective-permute-start.10 = (f32[8,130,1]{1,0,2:T(8,128)S(1)}, f32[8,130,1]{1,0,2:T(8,128)S(1)}, u32[]{:S(2)}, u32[]{:S(2)}) collective-permute-start(f32[8,130,1]{1,0,2:T(8,128)S(1)} %copy.17), channel_id=1, source_target_pairs={{0,4},{4,8},{8,12},{12,16},{16,20},{20,24},{24,28},{1,5},{5,9},{9,... | collective-permute-start | bytes 12488 | tf_op jit(solution)/shard_map/ppermute | solution.py:13
  67.1 1.3 collective-permute-start.11
  68.4 0.4 copy.18
  68.8 5.0 %collective-permute-done.11 = f32[8,130,1]{1,0,2:T(8,128)S(1)} collective-permute-done((f32[8,130,1]{1,0,2:T(8,128)S(1)}, f32[8,130,1]{1,0,2:T(8,128)S(1)}, u32[]{:S(2)}, u32[]{:S(2)}) %collective-permute-start.11) | collective-permute-done | bytes 4192 | tf_op jit(solution)/shard_map/ppermute | solution.py:16
  73.9 1.2 copy.20
  75.0 1.8 fusion.27
  76.8 1.3 collective-permute-start.13
  78.2 4.9 %collective-permute-start.12 = (f32[8,1,256]{2,0,1:T(8,128)S(1)}, f32[8,1,256]{2,0,1:T(8,128)S(1)}, u32[]{:S(2)}, u32[]{:S(2)}) collective-permute-start(f32[8,1,256]{2,0,1:T(8,128)S(1)} %get-tuple-element.20), channel_id=1, source_target_pairs={{0,32},{32,64},{64,96},{96,128},{128,160},{160,192},{192,224},{1,3... | collective-permute-start | bytes 24584 | tf_op jit(solution)/shard_map/ppermute | solution.py:13
  83.1 1.3 collective-permute-done.12
  84.5 1.0 fusion.48
  85.5 1.4 copy.21
  86.9 0.4 copy.23
  87.3 1.3 collective-permute-start.15
  88.6 5.4 %collective-permute-start.14 = (f32[8,130,1]{1,0,2:T(8,128)S(1)}, f32[8,130,1]{1,0,2:T(8,128)S(1)}, u32[]{:S(2)}, u32[]{:S(2)}) collective-permute-start(f32[8,130,1]{1,0,2:T(8,128)S(1)} %copy.21), channel_id=1, source_target_pairs={{0,4},{4,8},{8,12},{12,16},{16,20},{20,24},{24,28},{1,5},{5,9},{9,... | collective-permute-start | bytes 12488 | tf_op jit(solution)/shard_map/ppermute | solution.py:13
  94.1 0.7 fusion.57
  95.4 1.2 copy.22
  96.6 1.2 copy.24
  97.7 8.3 %fusion.20 = f32[8,128,256]{2,0,1:T(8,128)S(1)} fusion(f32[8,128,256]{2,0,1:T(8,128)S(1)} %fusion.34, f32[8,128,256]{2,0,1:T(8,128)} %copy-done, f32[8,1,256]{2,0,1:T(8,128)S(1)} %collective-permute-done.12, f32[8,1,256]{2,0,1:T(8,128)S(1)} %collective-permute-done.13, f32[8,130,1]{2,0,1:T(8,128)} %copy.24, f32[8,130,1]{2,0,1:T(8,128)} %copy.22, ...), kind=kLoop, calls=%fused_computation.33 | loop fusion | flops 6815744 | bytes 5562516 | tf_op jit(solution)/shard_map/add | solution.py:60
  106.1 1.3 collective-permute-start.17
  107.4 6.0 %collective-permute-start.16 = (f32[8,1,256]{2,0,1:T(8,128)S(1)}, f32[8,1,256]{2,0,1:T(8,128)S(1)}, u32[]{:S(2)}, u32[]{:S(2)}) collective-permute-start(f32[8,1,256]{2,0,1:T(8,128)S(1)} %get-tuple-element.18), channel_id=1, source_target_pairs={{0,32},{32,64},{64,96},{96,128},{128,160},{160,192},{192,224},{1,3... | collective-permute-start | bytes 24584 | tf_op jit(solution)/shard_map/ppermute | solution.py:13
  113.5 1.3 collective-permute-done.16
  115.1 0.4 copy.25
  115.4 4.8 %collective-permute-start.18 = (f32[8,130,1]{1,0,2:T(8,128)S(1)}, f32[8,130,1]{1,0,2:T(8,128)S(1)}, u32[]{:S(2)}, u32[]{:S(2)}) collective-permute-start(f32[8,130,1]{1,0,2:T(8,128)S(1)} %copy.25), channel_id=1, source_target_pairs={{0,4},{4,8},{8,12},{12,16},{16,20},{20,24},{24,28},{1,5},{5,9},{9,... | collective-permute-start | bytes 12488 | tf_op jit(solution)/shard_map/ppermute | solution.py:13
  120.6 1.5 collective-permute-start.19
  122.1 0.4 copy.26
  122.5 4.8 %collective-permute-done.19 = f32[8,130,1]{1,0,2:T(8,128)S(1)} collective-permute-done((f32[8,130,1]{1,0,2:T(8,128)S(1)}, f32[8,130,1]{1,0,2:T(8,128)S(1)}, u32[]{:S(2)}, u32[]{:S(2)}) %collective-permute-start.19) | collective-permute-done | bytes 4192 | tf_op jit(solution)/shard_map/ppermute | solution.py:16
  127.3 1.2 copy.28
  128.5 1.8 fusion.11
  130.3 1.5 pad_maximum_fusion
  131.8 71.7 %all-gather.2.cloned.1.call-done = f32[2,32,128,256]{3,1,2,0:T(8,128)} async-done(((f32[2,8,128,256]{3,1,2,0:T(8,128)}), f32[2,32,128,256]{3,1,2,0:T(8,128)}) %all-gather.2.cloned.1.call-update) | async-done | bytes 8388624 | tf_op jit(solution)/shard_map/all_gather | solution.py:66
  203.5 16.7 %fusion.3 = f32[2,32,64]{2,1,0:T(8,128)S(1)} fusion(f32[2,32,128,256]{3,1,2,0:T(8,128)} %all-gather.2.cloned.1.call-done, f32[64,128,256]{2,1,0:T(8,128)} %param.6), kind=kOutput, calls=%fused_computation.4 | convolution fusion | flops 1610612736 | bytes 16793600 | tf_op jit(solution)/shard_map/dot_general | solution.py:39
  220.2 34.9 %psum.14 = f32[2,32,64]{2,1,0:T(8,128)S(1)} all-reduce(f32[2,32,64]{2,1,0:T(8,128)S(1)} %fusion.3), channel_id=1, replica_groups=mesh['lx'=8,'ly'=8,'blk'=4] {'ly'}, use_global_device_ids=true, to_apply=%region_0.1 | all-reduce | flops 4096 | bytes 32768 | tf_op jit(solution)/shard_map/psum | solution.py:67
  255.1 30.2 %psum.15 = f32[2,32,64]{2,1,0:T(8,128)S(1)} all-reduce(f32[2,32,64]{2,1,0:T(8,128)S(1)} %psum.14), channel_id=1, replica_groups=mesh['lx'=8,'ly'=8,'blk'=4] {'lx'}, use_global_device_ids=true, to_apply=%region_1.2 | all-reduce | flops 4096 | bytes 32768 | tf_op jit(solution)/shard_map/psum | solution.py:67
  285.3 0.6 broadcast_multiply_fusion.2
  (35 shorter events, 1.9 us)
Async XLA Ops:
  6.5 197.0 %all-gather.2.cloned.1.call-start = ((), (), s32[]{:S(2)}) async-start(), calls=%async_computation | async-start | bytes 10485760 | tf_op jit(solution)/shard_map/all_gather | solution.py:66
  9.3 5.9 %collective-permute-start.1 = (f32[8,1,256]{2,0,1:T(8,128)S(1)}, f32[8,1,256]{2,0,1:T(8,128)S(1)}, u32[]{:S(2)}, u32[]{:S(2)}) collective-permute-start(f32[8,1,256]{2,0,1:T(8,128)S(1)} %get-tuple-element.25), channel_id=1, source_target_pairs={{32,0},{64,32},{96,64},{128,96},{160,128},{192,160},{224,192},{33,... | collective-permute-start | bytes 24584 | tf_op jit(solution)/shard_map/ppermute | solution.py:16
  10.6 5.9 %collective-permute-start = (f32[8,1,256]{2,0,1:T(8,128)S(1)}, f32[8,1,256]{2,0,1:T(8,128)S(1)}, u32[]{:S(2)}, u32[]{:S(2)}) collective-permute-start(f32[8,1,256]{2,0,1:T(8,128)S(1)} %get-tuple-element.26), channel_id=1, source_target_pairs={{0,32},{32,64},{64,96},{96,128},{128,160},{160,192},{192,224},{1,3... | collective-permute-start | bytes 24584 | tf_op jit(solution)/shard_map/ppermute | solution.py:13
  16.8 10.3 %copy-start.1 = (f32[128,256]{1,0:T(8,128)S(1)}, f32[128,256]{1,0:T(8,128)}, u32[]{:S(2)}) copy-start(f32[128,256]{1,0:T(8,128)} %param.7) | copy-start | bytes 393220
  17.5 8.4 %collective-permute-start.3 = (f32[8,130,1]{1,0,2:T(8,128)S(1)}, f32[8,130,1]{1,0,2:T(8,128)S(1)}, u32[]{:S(2)}, u32[]{:S(2)}) collective-permute-start(f32[8,130,1]{1,0,2:T(8,128)S(1)} %copy.11), channel_id=1, source_target_pairs={{4,0},{8,4},{12,8},{16,12},{20,16},{24,20},{28,24},{5,1},{9,5},{13... | collective-permute-start | bytes 12488 | tf_op jit(solution)/shard_map/ppermute | solution.py:16
  18.8 5.9 %collective-permute-start.2 = (f32[8,130,1]{1,0,2:T(8,128)S(1)}, f32[8,130,1]{1,0,2:T(8,128)S(1)}, u32[]{:S(2)}, u32[]{:S(2)}) collective-permute-start(f32[8,130,1]{1,0,2:T(8,128)S(1)} %copy.9), channel_id=1, source_target_pairs={{0,4},{4,8},{8,12},{12,16},{16,20},{20,24},{24,28},{1,5},{5,9},{9,... | collective-permute-start | bytes 12488 | tf_op jit(solution)/shard_map/ppermute | solution.py:13
  29.1 6.1 %collective-permute-start.5 = (f32[8,1,256]{2,0,1:T(8,128)S(1)}, f32[8,1,256]{2,0,1:T(8,128)S(1)}, u32[]{:S(2)}, u32[]{:S(2)}) collective-permute-start(f32[8,1,256]{2,0,1:T(8,128)S(1)} %get-tuple-element.23), channel_id=1, source_target_pairs={{32,0},{64,32},{96,64},{128,96},{160,128},{192,160},{224,192},{33,... | collective-permute-start | bytes 24584 | tf_op jit(solution)/shard_map/ppermute | solution.py:16
  30.4 6.2 %collective-permute-start.4 = (f32[8,1,256]{2,0,1:T(8,128)S(1)}, f32[8,1,256]{2,0,1:T(8,128)S(1)}, u32[]{:S(2)}, u32[]{:S(2)}) collective-permute-start(f32[8,1,256]{2,0,1:T(8,128)S(1)} %get-tuple-element.24), channel_id=1, source_target_pairs={{0,32},{32,64},{64,96},{96,128},{128,160},{160,192},{192,224},{1,3... | collective-permute-start | bytes 24584 | tf_op jit(solution)/shard_map/ppermute | solution.py:13
  39.4 8.7 %collective-permute-start.7 = (f32[8,130,1]{1,0,2:T(8,128)S(1)}, f32[8,130,1]{1,0,2:T(8,128)S(1)}, u32[]{:S(2)}, u32[]{:S(2)}) collective-permute-start(f32[8,130,1]{1,0,2:T(8,128)S(1)} %copy.15), channel_id=1, source_target_pairs={{4,0},{8,4},{12,8},{16,12},{20,16},{24,20},{28,24},{5,1},{9,5},{13... | collective-permute-start | bytes 12488 | tf_op jit(solution)/shard_map/ppermute | solution.py:16
  40.7 6.2 %collective-permute-start.6 = (f32[8,130,1]{1,0,2:T(8,128)S(1)}, f32[8,130,1]{1,0,2:T(8,128)S(1)}, u32[]{:S(2)}, u32[]{:S(2)}) collective-permute-start(f32[8,130,1]{1,0,2:T(8,128)S(1)} %copy.13), channel_id=1, source_target_pairs={{0,4},{4,8},{8,12},{12,16},{16,20},{20,24},{24,28},{1,5},{5,9},{9,... | collective-permute-start | bytes 12488 | tf_op jit(solution)/shard_map/ppermute | solution.py:13
  51.8 6.1 %collective-permute-start.9 = (f32[8,1,256]{2,0,1:T(8,128)S(1)}, f32[8,1,256]{2,0,1:T(8,128)S(1)}, u32[]{:S(2)}, u32[]{:S(2)}) collective-permute-start(f32[8,1,256]{2,0,1:T(8,128)S(1)} %get-tuple-element.21), channel_id=1, source_target_pairs={{32,0},{64,32},{96,64},{128,96},{160,128},{192,160},{224,192},{33,... | collective-permute-start | bytes 24584 | tf_op jit(solution)/shard_map/ppermute | solution.py:16
  53.1 6.2 %collective-permute-start.8 = (f32[8,1,256]{2,0,1:T(8,128)S(1)}, f32[8,1,256]{2,0,1:T(8,128)S(1)}, u32[]{:S(2)}, u32[]{:S(2)}) collective-permute-start(f32[8,1,256]{2,0,1:T(8,128)S(1)} %get-tuple-element.22), channel_id=1, source_target_pairs={{0,32},{32,64},{64,96},{96,128},{128,160},{160,192},{192,224},{1,3... | collective-permute-start | bytes 24584 | tf_op jit(solution)/shard_map/ppermute | solution.py:13
  61.8 6.6 %collective-permute-start.10 = (f32[8,130,1]{1,0,2:T(8,128)S(1)}, f32[8,130,1]{1,0,2:T(8,128)S(1)}, u32[]{:S(2)}, u32[]{:S(2)}) collective-permute-start(f32[8,130,1]{1,0,2:T(8,128)S(1)} %copy.17), channel_id=1, source_target_pairs={{0,4},{4,8},{8,12},{12,16},{16,20},{20,24},{24,28},{1,5},{5,9},{9,... | collective-permute-start | bytes 12488 | tf_op jit(solution)/shard_map/ppermute | solution.py:13
  67.1 6.7 %collective-permute-start.11 = (f32[8,130,1]{1,0,2:T(8,128)S(1)}, f32[8,130,1]{1,0,2:T(8,128)S(1)}, u32[]{:S(2)}, u32[]{:S(2)}) collective-permute-start(f32[8,130,1]{1,0,2:T(8,128)S(1)} %copy.19), channel_id=1, source_target_pairs={{4,0},{8,4},{12,8},{16,12},{20,16},{24,20},{28,24},{5,1},{9,5},{13... | collective-permute-start | bytes 12488 | tf_op jit(solution)/shard_map/ppermute | solution.py:16
  76.8 7.7 %copy-start = (f32[8,128,256]{2,0,1:T(8,128)}, f32[8,128,256]{2,0,1:T(8,128)S(1)}, u32[]{:S(2)}) copy-start(f32[8,128,256]{2,0,1:T(8,128)S(1)} %fusion.27) | copy-start | bytes 3145732
  76.8 6.2 %collective-permute-start.13 = (f32[8,1,256]{2,0,1:T(8,128)S(1)}, f32[8,1,256]{2,0,1:T(8,128)S(1)}, u32[]{:S(2)}, u32[]{:S(2)}) collective-permute-start(f32[8,1,256]{2,0,1:T(8,128)S(1)} %get-tuple-element.19), channel_id=1, source_target_pairs={{32,0},{64,32},{96,64},{128,96},{160,128},{192,160},{224,192},{33,... | collective-permute-start | bytes 24584 | tf_op jit(solution)/shard_map/ppermute | solution.py:16
  78.2 6.3 %collective-permute-start.12 = (f32[8,1,256]{2,0,1:T(8,128)S(1)}, f32[8,1,256]{2,0,1:T(8,128)S(1)}, u32[]{:S(2)}, u32[]{:S(2)}) collective-permute-start(f32[8,1,256]{2,0,1:T(8,128)S(1)} %get-tuple-element.20), channel_id=1, source_target_pairs={{0,32},{32,64},{64,96},{96,128},{128,160},{160,192},{192,224},{1,3... | collective-permute-start | bytes 24584 | tf_op jit(solution)/shard_map/ppermute | solution.py:13
  85.5 8.5 %copy-start.2 = (f32[5]{0:T(128)S(1)}, f32[5]{0:T(128)}, u32[]{:S(2)}) copy-start(f32[5]{0:T(128)} %param.9) | copy-start | bytes 64
  87.3 9.3 %collective-permute-start.15 = (f32[8,130,1]{1,0,2:T(8,128)S(1)}, f32[8,130,1]{1,0,2:T(8,128)S(1)}, u32[]{:S(2)}, u32[]{:S(2)}) collective-permute-start(f32[8,130,1]{1,0,2:T(8,128)S(1)} %copy.23), channel_id=1, source_target_pairs={{4,0},{8,4},{12,8},{16,12},{20,16},{24,20},{28,24},{5,1},{9,5},{13... | collective-permute-start | bytes 12488 | tf_op jit(solution)/shard_map/ppermute | solution.py:16
  88.6 6.8 %collective-permute-start.14 = (f32[8,130,1]{1,0,2:T(8,128)S(1)}, f32[8,130,1]{1,0,2:T(8,128)S(1)}, u32[]{:S(2)}, u32[]{:S(2)}) collective-permute-start(f32[8,130,1]{1,0,2:T(8,128)S(1)} %copy.21), channel_id=1, source_target_pairs={{0,4},{4,8},{8,12},{12,16},{16,20},{20,24},{24,28},{1,5},{5,9},{9,... | collective-permute-start | bytes 12488 | tf_op jit(solution)/shard_map/ppermute | solution.py:13
  106.1 7.3 %collective-permute-start.17 = (f32[8,1,256]{2,0,1:T(8,128)S(1)}, f32[8,1,256]{2,0,1:T(8,128)S(1)}, u32[]{:S(2)}, u32[]{:S(2)}) collective-permute-start(f32[8,1,256]{2,0,1:T(8,128)S(1)} %get-tuple-element.17), channel_id=1, source_target_pairs={{32,0},{64,32},{96,64},{128,96},{160,128},{192,160},{224,192},{33,... | collective-permute-start | bytes 24584 | tf_op jit(solution)/shard_map/ppermute | solution.py:16
  107.4 7.4 %collective-permute-start.16 = (f32[8,1,256]{2,0,1:T(8,128)S(1)}, f32[8,1,256]{2,0,1:T(8,128)S(1)}, u32[]{:S(2)}, u32[]{:S(2)}) collective-permute-start(f32[8,1,256]{2,0,1:T(8,128)S(1)} %get-tuple-element.18), channel_id=1, source_target_pairs={{0,32},{32,64},{64,96},{96,128},{128,160},{160,192},{192,224},{1,3... | collective-permute-start | bytes 24584 | tf_op jit(solution)/shard_map/ppermute | solution.py:13
  115.4 6.7 %collective-permute-start.18 = (f32[8,130,1]{1,0,2:T(8,128)S(1)}, f32[8,130,1]{1,0,2:T(8,128)S(1)}, u32[]{:S(2)}, u32[]{:S(2)}) collective-permute-start(f32[8,130,1]{1,0,2:T(8,128)S(1)} %copy.25), channel_id=1, source_target_pairs={{0,4},{4,8},{8,12},{12,16},{16,20},{20,24},{24,28},{1,5},{5,9},{9,... | collective-permute-start | bytes 12488 | tf_op jit(solution)/shard_map/ppermute | solution.py:13
  120.6 6.7 %collective-permute-start.19 = (f32[8,130,1]{1,0,2:T(8,128)S(1)}, f32[8,130,1]{1,0,2:T(8,128)S(1)}, u32[]{:S(2)}, u32[]{:S(2)}) collective-permute-start(f32[8,130,1]{1,0,2:T(8,128)S(1)} %copy.27), channel_id=1, source_target_pairs={{4,0},{8,4},{12,8},{16,12},{20,16},{24,20},{28,24},{5,1},{9,5},{13... | collective-permute-start | bytes 12488 | tf_op jit(solution)/shard_map/ppermute | solution.py:16
Sparse Core Ops, SparseCore 0:
  131.9 71.4 all-gather.1
